TPU v7x, 32 devices: a whole 2x2x4 slice. The times are simulated.
32 devices in a mesh: section: 4 (over y, x), seq: 8 (over z, core).
Axes of the slice: x: 2, y: 2, z: 4, core: 2. Of those that a mesh axis runs over, the one named last changes fastest.
Arguments:
- inflow: bfloat16 [4, 512, 4096], P('section', 'seq'), may hold values from -6 to 6
- fresh: bfloat16 [1, 512, 4096], P(None, 'seq'), may hold values from -6 to 6
- proj_weight: bfloat16 [4, 4096, 640], P('section'), may hold values from -0.09375 to 0.09375
- xz_weight: bfloat16 [4, 4096, 2, 4096], P('section', None, None, 'seq'), may hold values from -0.09375 to 0.09375
- conv_weight: float32 [4, 4, 4608], P('section'), may hold values from -3 to 3
- conv_bias: float32 [4, 4608], P('section'), may hold values from -3 to 3
- step_bias: float32 [4, 128], P('section'), may hold values from -3 to 0
- decay_log: float32 [4, 128], P('section'), may hold values from -7 to -1
- skip_weight: float32 [4, 128], P('section'), may hold values from 0.5 to 1.5
- norm_gain: float32 [4, 4096], P('section'), may hold values from 0.5 to 1.5
- out_weight: bfloat16 [4, 4096, 4096], P('section', 'seq'), may hold values from -0.09375 to 0.09375
Outputs:
- section_outputs: float32 [4, 2, 512, 4096], P('section', None, 'seq')
All inputs are finite; a program needn't handle non-finite values.
Results may differ from a plain program's by a relative error of at most 0.014.
Values may be sent and summed in bfloat16 or wider, within the bound.
No kernel may reach another device: no remote copies, remote signals or barrier semaphores. Data moves between devices by JAX's collectives and lax.ppermute only.
A program may use at most 128 MiB of HBM per device.

v0:
```python
import jax
import jax.numpy as jnp
from jax import lax
from jax.sharding import PartitionSpec as P

HEADS = 128
HEAD_DIM = 32
STATE = 64
GROUPS = 4
CONV = 4
BLOCK = 128


def shifted(value, axis, steps):
    count = lax.axis_size(axis)
    leading, last = (max(0, -steps), min(count, count - steps))
    return lax.ppermute(value, axis, [(source, source + steps) for source in range(leading, last)])


def run_block(state, pieces):
    x_block, b_block, c_block, step_block, decay_block = pieces
    cumulus = jnp.cumsum(decay_block, axis=0)
    scores = jnp.einsum("qgn,kgn->gqk", c_block, b_block, preferred_element_type=jnp.float32)
    along = jnp.moveaxis(cumulus, 0, 2)
    row_count = cumulus.shape[0]
    row_index = lax.broadcasted_iota(jnp.int32, (row_count, row_count), 0)
    col_index = lax.broadcasted_iota(jnp.int32, (row_count, row_count), 1)
    log_gap = jnp.where(row_index >= col_index, along[..., :, None] - along[..., None, :], -1e30)
    step_along = jnp.moveaxis(step_block, 0, 2)
    mixing = (scores[:, None] * jnp.exp(log_gap) * step_along[..., None, :]).astype(jnp.bfloat16)
    diagonal_out = jnp.einsum(
        "gjqk,kgjp->qgjp", mixing, x_block, preferred_element_type=jnp.float32
    )
    block_total = cumulus[-1]
    weighted = (
        x_block.astype(jnp.float32) * (jnp.exp(block_total[None] - cumulus) * step_block)[..., None]
    ).astype(jnp.bfloat16)
    block_state = jnp.einsum(
        "kgjp,kgn->gjpn", weighted, b_block, preferred_element_type=jnp.float32
    )
    entering = state.astype(jnp.bfloat16)
    off_out = (
        jnp.einsum("qgn,gjpn->qgjp", c_block, entering, preferred_element_type=jnp.float32)
        * jnp.exp(cumulus)[..., None]
    )
    new_state = jnp.exp(block_total)[..., None, None] * state + block_state
    return (new_state, diagonal_out + off_out)


def on_device(
    inflow,
    fresh,
    proj_weight,
    xz_weight,
    conv_weight,
    conv_bias,
    step_bias,
    decay_log,
    skip_weight,
    norm_gain,
    out_weight,
):
    group_size = lax.axis_size("seq")
    position = lax.axis_index("section")
    member = lax.axis_index("seq")
    tokens, width = (inflow.shape[1], inflow.shape[2])
    length = tokens * group_size
    inner = HEADS * HEAD_DIM
    heads_dev = HEADS // group_size
    chan_dev = heads_dev * HEAD_DIM
    bc_width = GROUPS * STATE
    per_group = HEADS // GROUPS
    head_start = member * heads_dev
    group_index = head_start // per_group
    b_start = group_index * STATE
    c_start = bc_width + group_index * STATE
    dt_start = 2 * bc_width + head_start
    xz_local = xz_weight[0].reshape(width, 2 * chan_dev)
    full_proj = proj_weight[0]

    def own_channels(table):
        last = table.ndim - 1
        return jnp.concatenate(
            [
                lax.dynamic_slice_in_dim(table, head_start * HEAD_DIM, chan_dev, last),
                lax.dynamic_slice_in_dim(table, inner + b_start, STATE, last),
                lax.dynamic_slice_in_dim(table, inner + c_start, STATE, last),
            ],
            axis=last,
        )

    taps_own = own_channels(conv_weight[0])
    offset_own = own_channels(conv_bias[0])
    bias_own = lax.dynamic_slice_in_dim(step_bias[0], head_start, heads_dev)
    rate_own = -jnp.exp(lax.dynamic_slice_in_dim(decay_log[0], head_start, heads_dev))
    skip_own = lax.dynamic_slice_in_dim(skip_weight[0], head_start, heads_dev)
    gain_own = lax.dynamic_slice_in_dim(norm_gain[0], head_start * HEAD_DIM, chan_dev)
    out_local = out_weight[0]
    group_mask = (lax.broadcasted_iota(jnp.int32, (GROUPS, 1), 0) == group_index).astype(
        jnp.float32
    )
    own_weight = jnp.concatenate(
        [
            xz_local,
            lax.dynamic_slice_in_dim(full_proj, b_start, STATE, 1),
            lax.dynamic_slice_in_dim(full_proj, c_start, STATE, 1),
            lax.dynamic_slice_in_dim(full_proj, dt_start, heads_dev, 1),
        ],
        axis=1,
    )

    def layer(shard):
        projected = jnp.dot(
            lax.all_gather(shard, "seq", axis=0, tiled=True),
            own_weight,
            preferred_element_type=jnp.float32,
        ).astype(jnp.bfloat16)
        gate_z = projected[:, :chan_dev]
        joined = projected[:, chan_dev : 2 * chan_dev + 2 * STATE]
        padded = jnp.concatenate(
            [jnp.zeros((CONV - 1, joined.shape[1]), jnp.bfloat16), joined], axis=0
        )
        conv_sum = offset_own + taps_own[0] * padded[0:length].astype(jnp.float32)
        for offset in range(1, CONV):
            conv_sum = conv_sum + taps_own[offset] * padded[offset : offset + length].astype(
                jnp.float32
            )
        convolved = jax.nn.silu(conv_sum).astype(jnp.bfloat16)
        block_count = length // BLOCK
        x_part = convolved[:, :chan_dev]
        x_blocks = x_part.reshape(block_count, BLOCK, 1, heads_dev, HEAD_DIM)
        b_blocks = convolved[:, chan_dev : chan_dev + STATE].reshape(block_count, BLOCK, 1, STATE)
        c_blocks = convolved[:, chan_dev + STATE :].reshape(block_count, BLOCK, 1, STATE)
        step_size = jax.nn.softplus(
            projected[:, 2 * chan_dev + 2 * STATE :].astype(jnp.float32) + bias_own
        )
        log_decay = rate_own * step_size
        step_blocks = step_size.reshape(block_count, BLOCK, 1, heads_dev)
        decay_blocks = log_decay.reshape(block_count, BLOCK, 1, heads_dev)
        start_state = jnp.zeros((1, heads_dev, HEAD_DIM, STATE), jnp.float32)
        _, scanned = lax.scan(
            run_block, start_state, (x_blocks, b_blocks, c_blocks, step_blocks, decay_blocks)
        )
        mixed = scanned.reshape(length, heads_dev, HEAD_DIM) + skip_own[:, None] * x_part.reshape(
            length, heads_dev, HEAD_DIM
        ).astype(jnp.float32)
        gated = mixed.reshape(length, chan_dev) * jax.nn.silu(gate_z.astype(jnp.float32))
        own_squares = jnp.sum(gated * gated, axis=1)
        summed_squares = lax.psum(group_mask * own_squares[None, :], "seq")
        mean_square = jnp.sum(summed_squares * group_mask, axis=0) / (inner // GROUPS)
        normed = (gated * lax.rsqrt(mean_square + 1e-05)[:, None] * gain_own).astype(jnp.bfloat16)
        return lax.psum_scatter(
            jnp.dot(normed, out_local, preferred_element_type=jnp.float32),
            "seq",
            scatter_dimension=0,
            tiled=True,
        )

    results = [layer(inflow[0])]
    passed = shifted(results[-1].astype(jnp.bfloat16), "section", 1)
    entering_rows = jnp.where(position == 0, fresh[0], passed)
    results.append(layer(entering_rows))
    return jnp.stack(results)[None]


def solution(mesh):
    placed = (
        P("section", "seq", None),
        P(None, "seq", None),
        P("section", None, None),
        P("section", None, None, "seq"),
        P("section", None, None),
        P("section", None),
        P("section", None),
        P("section", None),
        P("section", None),
        P("section", None),
        P("section", "seq", None),
    )
    return jax.shard_map(
        on_device,
        mesh=mesh,
        in_specs=placed,
        out_specs=P("section", None, "seq", None),
        check_vma=False,
    )
```

profile of v0, /device:TPU:0, one launch (start us, length us, event | category | flops | bytes accessed | tf_op | source)
XLA Modules:
  0.0 464.4 jit_solution(18057231383627719839)
XLA Ops:
  7.4 9.4 %copy.88 = bf16[512,8,2,512]{3,1,2,0:T(8,128)(2,1)} copy(bf16[512,8,2,512]{3,2,1,0:T(2,128)(2,1)} %bitcast.287) | data formatting | bytes 16777216
  17.6 1.6 dynamic-slice_bitcast_fusion
  19.2 2.5 dynamic-slice_bitcast_fusion.1
  21.8 15.5 %concatenate.15 = bf16[4096,1168]{1,0:T(8,128)(2,1)} concatenate(bf16[4096,1024]{1,0:T(8,128)(2,1)} %bitcast.282, bf16[4096,64]{1,0:T(8,128)(2,1)S(1)} %get-tuple-element.240, bf16[4096,64]{1,0:T(8,128)(2,1)S(1)} %get-tuple-element.239, bf16[4096,16]{1,0:T(8,128)(2,1)S(1)} %dynamic-slice_bitcast_fusion), dimensions={1} | concatenate | bytes 19136512 | tf_op jit(solution)/shard_map/concatenate | solution.py:102
  41.7 16.9 %all-gather.6.cloned.1.call-done = bf16[1,512,4096]{2,1,0:T(8,128)(2,1)} async-done(((bf16[1,64,4096]{2,1,0:T(8,128)(2,1)}), bf16[1,512,4096]{2,1,0:T(8,128)(2,1)}) %all-gather.6.cloned.1.call-update) | async-done | bytes 4194320 | tf_op jit(solution)/shard_map/all_gather | solution.py:114
  58.6 10.6 %fusion.79 = bf16[512,1168]{0,1:T(8,128)(2,1)S(1)} fusion(bf16[4096,1168]{1,0:T(8,128)(2,1)} %concatenate.15, bf16[1,512,4096]{2,1,0:T(8,128)(2,1)} %all-gather.6.cloned.1.call-done), kind=kOutput, calls=%fused_computation.96 | convolution fusion | flops 4899545088 | bytes 14958592 | tf_op jit(solution)/shard_map/dot_general | solution.py:113
  69.2 1.5 multiply_convert_fusion.7
  73.2 38.5 %while.26 = (s32[]{:T(128)}, f32[1,16,32,64]{3,2,1,0:T(8,128)S(1)}, f32[4,128,1,16,32]{1,0,4,3,2:T(4,128)S(1)}, f32[4,128,1,16]{3,1,2,0:T(8,128)}, bf16[4,128,1,...) while((s32[]{:T(128)}, f32[1,16,32,64]{3,2,1,0:T(8,128)S(1)}, ...), condition=%wide.region_2.3_spmd.clone, body=%wide.region_0.2_spmd.clone.sunk | while | flops 37701632 | bytes 2641344 | solution.py:141
  77.3 5.3 %dynamic_update_slice.11 = f32[4,128,1,16,32]{1,0,4,3,2:T(4,128)S(1)} dynamic-update-slice(f32[4,128,1,16,32]{1,0,4,3,2:T(4,128)S(1)} %get-tuple-element.377, f32[1,128,1,16,32]{1,0,4,3,2:T(1,128)S(1)} %bitcast.288, s32[]{:T(128)} %get-tuple-element.375, s32[]{:T(128)} %constant.98.clone.1..sunk, s32[]{:T(128)} %constant.98.clone.1..sunk, s32[]{:T(128)} %constant.98.clone.1..sunk, ...) | dynamic-update-slice | bytes 524292 | tf_op jit(solution)/shard_map/while/body/jit(dynamic_update_index_in_dim)/dynamic_update_slice | solution.py:141
  86.9 5.3 %dynamic_update_slice.11 = f32[4,128,1,16,32]{1,0,4,3,2:T(4,128)S(1)} dynamic-update-slice(f32[4,128,1,16,32]{1,0,4,3,2:T(4,128)S(1)} %get-tuple-element.377, f32[1,128,1,16,32]{1,0,4,3,2:T(1,128)S(1)} %bitcast.288, s32[]{:T(128)} %get-tuple-element.375, s32[]{:T(128)} %constant.98.clone.1..sunk, s32[]{:T(128)} %constant.98.clone.1..sunk, s32[]{:T(128)} %constant.98.clone.1..sunk, ...) | dynamic-update-slice | bytes 524292 | tf_op jit(solution)/shard_map/while/body/jit(dynamic_update_index_in_dim)/dynamic_update_slice | solution.py:141
  96.5 5.3 %dynamic_update_slice.11 = f32[4,128,1,16,32]{1,0,4,3,2:T(4,128)S(1)} dynamic-update-slice(f32[4,128,1,16,32]{1,0,4,3,2:T(4,128)S(1)} %get-tuple-element.377, f32[1,128,1,16,32]{1,0,4,3,2:T(1,128)S(1)} %bitcast.288, s32[]{:T(128)} %get-tuple-element.375, s32[]{:T(128)} %constant.98.clone.1..sunk, s32[]{:T(128)} %constant.98.clone.1..sunk, s32[]{:T(128)} %constant.98.clone.1..sunk, ...) | dynamic-update-slice | bytes 524292 | tf_op jit(solution)/shard_map/while/body/jit(dynamic_update_index_in_dim)/dynamic_update_slice | solution.py:141
  106.2 5.3 %dynamic_update_slice.11 = f32[4,128,1,16,32]{1,0,4,3,2:T(4,128)S(1)} dynamic-update-slice(f32[4,128,1,16,32]{1,0,4,3,2:T(4,128)S(1)} %get-tuple-element.377, f32[1,128,1,16,32]{1,0,4,3,2:T(1,128)S(1)} %bitcast.288, s32[]{:T(128)} %get-tuple-element.375, s32[]{:T(128)} %constant.98.clone.1..sunk, s32[]{:T(128)} %constant.98.clone.1..sunk, s32[]{:T(128)} %constant.98.clone.1..sunk, ...) | dynamic-update-slice | bytes 524292 | tf_op jit(solution)/shard_map/while/body/jit(dynamic_update_index_in_dim)/dynamic_update_slice | solution.py:141
  111.8 1.5 multiply_reduce_fusion.1
  113.3 15.2 %psum.14 = f32[4,512]{1,0:T(4,128)S(1)} all-reduce(f32[4,512]{1,0:T(4,128)S(1)} %broadcast_multiply_fusion.3), channel_id=1, replica_groups=mesh['section'=4,'seq'=8] {'seq'}, use_global_device_ids=true, to_apply=%region_4.5 | all-reduce | flops 2048 | bytes 16384 | tf_op jit(solution)/shard_map/psum | solution.py:149
  128.7 8.0 %fusion.72 = f32[512,4096]{1,0:T(8,128)} fusion(bf16[1,512,4096]{2,1,0:T(8,128)(2,1)} %param.25, f32[512,512]{0,1:T(8,128)S(1)} %get-tuple-element.236, f32[512]{0:T(512)S(1)} %bitcast.300, f32[512]{0:T(512)S(1)} %add_rsqrt_fusion.1), kind=kOutput, calls=%fused_computation.90 | convolution fusion | flops 2148270080 | bytes 13635584 | tf_op jit(solution)/shard_map/dot_general | solution.py:153
  136.7 87.5 %reduce-scatter.3.cloned.1.call-done = f32[64,4096]{1,0:T(8,128)} async-done(((f32[512,4096]{1,0:T(8,128)}), f32[64,4096]{1,0:T(8,128)}) %reduce-scatter.3.cloned.1.call-update) | async-done | bytes 1048592 | tf_op jit(solution)/shard_map/reduce_scatter | solution.py:152
  224.3 1.3 convert_element_type.138
  225.5 3.4 collective-permute-start
  228.9 9.2 %collective-permute-done = bf16[64,4096]{1,0:T(8,128)(2,1)S(1)} collective-permute-done((bf16[64,4096]{1,0:T(8,128)(2,1)S(1)}, bf16[64,4096]{1,0:T(8,128)(2,1)S(1)}, u32[]{:S(2)}, u32[]{:S(2)}) %collective-permute-start) | collective-permute-done | bytes 524320 | tf_op jit(solution)/shard_map/ppermute | solution.py:17
  239.1 48.3 %all-gather.4.cloned.1.call-done = bf16[512,4096]{1,0:T(8,128)(2,1)} async-done(((bf16[64,4096]{1,0:T(8,128)(2,1)}), bf16[512,4096]{1,0:T(8,128)(2,1)}) %all-gather.4.cloned.1.call-update) | async-done | bytes 4194320 | tf_op jit(solution)/shard_map/all_gather | solution.py:114
  287.4 12.7 %convolution_convert_fusion = bf16[512,1168]{0,1:T(8,128)(2,1)S(1)} fusion(bf16[512,4096]{1,0:T(8,128)(2,1)} %all-gather.4.cloned.1.call-done, bf16[4096,1168]{1,0:T(8,128)(2,1)} %concatenate.15), kind=kOutput, calls=%fused_computation.94 | convolution fusion | flops 4899545088 | bytes 14958592 | tf_op jit(solution)/shard_map/dot_general | solution.py:113
  300.9 1.5 multiply_convert_fusion.6
  304.2 38.5 %while.27 = (s32[]{:T(128)}, f32[1,16,32,64]{3,2,1,0:T(8,128)S(1)}, f32[4,128,1,16,32]{1,0,4,3,2:T(4,128)S(1)}, f32[4,128,1,16]{3,1,2,0:T(8,128)}, bf16[4,128,1,...) while((s32[]{:T(128)}, f32[1,16,32,64]{3,2,1,0:T(8,128)S(1)}, ...), condition=%wide.region_9.10_spmd.clone, body=%wide.region_7.9_spmd.clone.sunk | while | flops 37701632 | bytes 2641344 | solution.py:141
  308.2 5.3 %dynamic_update_slice.12 = f32[4,128,1,16,32]{1,0,4,3,2:T(4,128)S(1)} dynamic-update-slice(f32[4,128,1,16,32]{1,0,4,3,2:T(4,128)S(1)} %get-tuple-element.407, f32[1,128,1,16,32]{1,0,4,3,2:T(1,128)S(1)} %bitcast.289, s32[]{:T(128)} %get-tuple-element.405, s32[]{:T(128)} %constant.98.clone.1..sunk.1, s32[]{:T(128)} %constant.98.clone.1..sunk.1, s32[]{:T(128)} %constant.98.clone.1..sunk.1, ...) | dynamic-update-slice | bytes 524292 | tf_op jit(solution)/shard_map/while/body/jit(dynamic_update_index_in_dim)/dynamic_update_slice | solution.py:141
  317.8 5.3 %dynamic_update_slice.12 = f32[4,128,1,16,32]{1,0,4,3,2:T(4,128)S(1)} dynamic-update-slice(f32[4,128,1,16,32]{1,0,4,3,2:T(4,128)S(1)} %get-tuple-element.407, f32[1,128,1,16,32]{1,0,4,3,2:T(1,128)S(1)} %bitcast.289, s32[]{:T(128)} %get-tuple-element.405, s32[]{:T(128)} %constant.98.clone.1..sunk.1, s32[]{:T(128)} %constant.98.clone.1..sunk.1, s32[]{:T(128)} %constant.98.clone.1..sunk.1, ...) | dynamic-update-slice | bytes 524292 | tf_op jit(solution)/shard_map/while/body/jit(dynamic_update_index_in_dim)/dynamic_update_slice | solution.py:141
  327.5 5.3 %dynamic_update_slice.12 = f32[4,128,1,16,32]{1,0,4,3,2:T(4,128)S(1)} dynamic-update-slice(f32[4,128,1,16,32]{1,0,4,3,2:T(4,128)S(1)} %get-tuple-element.407, f32[1,128,1,16,32]{1,0,4,3,2:T(1,128)S(1)} %bitcast.289, s32[]{:T(128)} %get-tuple-element.405, s32[]{:T(128)} %constant.98.clone.1..sunk.1, s32[]{:T(128)} %constant.98.clone.1..sunk.1, s32[]{:T(128)} %constant.98.clone.1..sunk.1, ...) | dynamic-update-slice | bytes 524292 | tf_op jit(solution)/shard_map/while/body/jit(dynamic_update_index_in_dim)/dynamic_update_slice | solution.py:141
  337.1 5.3 %dynamic_update_slice.12 = f32[4,128,1,16,32]{1,0,4,3,2:T(4,128)S(1)} dynamic-update-slice(f32[4,128,1,16,32]{1,0,4,3,2:T(4,128)S(1)} %get-tuple-element.407, f32[1,128,1,16,32]{1,0,4,3,2:T(1,128)S(1)} %bitcast.289, s32[]{:T(128)} %get-tuple-element.405, s32[]{:T(128)} %constant.98.clone.1..sunk.1, s32[]{:T(128)} %constant.98.clone.1..sunk.1, s32[]{:T(128)} %constant.98.clone.1..sunk.1, ...) | dynamic-update-slice | bytes 524292 | tf_op jit(solution)/shard_map/while/body/jit(dynamic_update_index_in_dim)/dynamic_update_slice | solution.py:141
  342.7 1.5 multiply_reduce_fusion
  344.3 15.2 %psum.15 = f32[4,512]{1,0:T(4,128)S(1)} all-reduce(f32[4,512]{1,0:T(4,128)S(1)} %broadcast_multiply_fusion.2), channel_id=1, replica_groups=mesh['section'=4,'seq'=8] {'seq'}, use_global_device_ids=true, to_apply=%region_11.12 | all-reduce | flops 2048 | bytes 16384 | tf_op jit(solution)/shard_map/psum | solution.py:149
  359.6 7.9 %fusion.70 = f32[512,4096]{1,0:T(8,128)} fusion(bf16[1,512,4096]{2,1,0:T(8,128)(2,1)} %param.25, f32[512,512]{0,1:T(8,128)S(1)} %get-tuple-element.234, f32[512]{0:T(512)S(1)} %add_rsqrt_fusion, f32[512]{0:T(512)S(1)} %bitcast.301), kind=kOutput, calls=%fused_computation.88 | convolution fusion | flops 2148270080 | bytes 13635584 | tf_op jit(solution)/shard_map/dot_general | solution.py:153
  367.6 87.6 %reduce-scatter.5.cloned.1.call-done = f32[64,4096]{1,0:T(8,128)} async-done(((f32[512,4096]{1,0:T(8,128)}), f32[64,4096]{1,0:T(8,128)}) %reduce-scatter.5.cloned.1.call-update) | async-done | bytes 1048592 | tf_op jit(solution)/shard_map/reduce_scatter | solution.py:152
  455.1 2.7 maximum_bitcast_fusion
  (222 shorter events, 46.3 us)
Async XLA Ops:
  6.5 32.8 %copy-start = (f32[1,4096]{1,0:T(1,128)S(1)}, f32[1,4096]{1,0:T(1,128)}, u32[]{:S(2)}) copy-start(f32[1,4096]{1,0:T(1,128)} %param.24) | copy-start | bytes 49156
  6.5 52.0 %all-gather.6.cloned.1.call-start = ((), (), s32[]{:S(2)}) async-start(), calls=%async_computation.5 | async-start | bytes 4718592 | tf_op jit(solution)/shard_map/all_gather | solution.py:114
  7.3 217.0 %reduce-scatter.3.cloned.1.call-start = ((), (), s32[]{:S(2)}) async-start(), calls=%async_computation.2 | async-start | bytes 9437184 | tf_op jit(solution)/shard_map/reduce_scatter | solution.py:152
  7.3 9.4 %copy-start.26 = (f32[1,128]{1,0:T(1,128)S(1)}, f32[1,128]{1,0:T(1,128)}, u32[]{:S(2)}) copy-start(f32[1,128]{1,0:T(1,128)} %param.23) | copy-start | bytes 1540
  21.8 16.1 %copy-start.24 = (f32[1,128]{1,0:T(1,128)S(1)}, f32[1,128]{1,0:T(1,128)}, u32[]{:S(2)}) copy-start(f32[1,128]{1,0:T(1,128)} %param.21) | copy-start | bytes 1540
  21.8 16.1 %copy-start.25 = (f32[1,128]{1,0:T(1,128)S(1)}, f32[1,128]{1,0:T(1,128)}, u32[]{:S(2)}) copy-start(f32[1,128]{1,0:T(1,128)} %param.22) | copy-start | bytes 1540
  37.9 33.2 %copy-start.20 = (f32[16]{0:T(128)}, f32[16]{0:T(128)S(1)}, u32[]{:S(2)}) copy-start(f32[16]{0:T(128)S(1)} %get-tuple-element.253) | copy-start | bytes 196
  37.9 33.2 %copy-start.22 = (f32[16]{0:T(128)}, f32[16]{0:T(128)S(1)}, u32[]{:S(2)}) copy-start(f32[16]{0:T(128)S(1)} %get-tuple-element.254) | copy-start | bytes 196
  40.8 28.4 %copy-start.8 = (f32[640]{0:T(1024)}, f32[640]{0:T(1024)S(1)}, u32[]{:S(2)}) copy-start(f32[640]{0:T(1024)S(1)} %pad_maximum_fusion.1) | copy-start | bytes 7684
  41.6 27.6 %copy-start.10 = (f32[640]{0:T(1024)}, f32[640]{0:T(1024)S(1)}, u32[]{:S(2)}) copy-start(f32[640]{0:T(1024)S(1)} %get-tuple-element.193) | copy-start | bytes 7684
  41.6 27.6 %copy-start.12 = (f32[640]{0:T(1024)}, f32[640]{0:T(1024)S(1)}, u32[]{:S(2)}) copy-start(f32[640]{0:T(1024)S(1)} %get-tuple-element.194) | copy-start | bytes 7684
  41.6 27.6 %copy-start.14 = (f32[640]{0:T(1024)}, f32[640]{0:T(1024)S(1)}, u32[]{:S(2)}) copy-start(f32[640]{0:T(1024)S(1)} %get-tuple-element.195) | copy-start | bytes 7684
  41.6 27.6 %copy-start.16 = (f32[640]{0:T(1024)}, f32[640]{0:T(1024)S(1)}, u32[]{:S(2)}) copy-start(f32[640]{0:T(1024)S(1)} %get-tuple-element.196) | copy-start | bytes 7684
  69.1 1.7 copy-start.4
  111.7 1.5 copy-start.18
  111.7 16.9 %copy-start.6 = (f32[1,512]{1,0:T(1,128)S(1)}, f32[1,512]{1,0:T(1,128)}, u32[]{:S(2)}) copy-start(f32[1,512]{1,0:T(1,128)} %constant_dynamic-slice_fusion.4) | copy-start | bytes 6148
  136.7 101.5 %copy-start.5 = (bf16[1,64,4096]{2,1,0:T(8,128)(2,1)S(1)}, bf16[1,64,4096]{2,1,0:T(8,128)(2,1)}, u32[]{:S(2)}) copy-start(bf16[1,64,4096]{2,1,0:T(8,128)(2,1)} %param.16) | copy-start | bytes 1572868
  136.7 150.8 %all-gather.4.cloned.1.call-start = ((), (), s32[]{:S(2)}) async-start(), calls=%async_computation.3 | async-start | bytes 4718592 | tf_op jit(solution)/shard_map/all_gather | solution.py:114
  225.5 12.7 %collective-permute-start = (bf16[64,4096]{1,0:T(8,128)(2,1)S(1)}, bf16[64,4096]{1,0:T(8,128)(2,1)S(1)}, u32[]{:S(2)}, u32[]{:S(2)}) collective-permute-start(bf16[64,4096]{1,0:T(8,128)(2,1)S(1)} %convert_element_type.138), channel_id=1, source_target_pairs={{0,8},{8,16},{16,24},{1,9},{9,17},{17,25},{2,10},{10,18},{18,26},{... | collective-permute-start | bytes 1572872 | tf_op jit(solution)/shard_map/ppermute | solution.py:17
  239.1 216.1 %reduce-scatter.5.cloned.1.call-start = ((), (), s32[]{:S(2)}) async-start(), calls=%async_computation.4 | async-start | bytes 9437184 | tf_op jit(solution)/shard_map/reduce_scatter | solution.py:152
  300.2 2.4 copy-start.3
  300.2 0.7 copy-start.9
  300.2 0.7 copy-start.11
  300.2 0.7 copy-start.13
  300.2 0.7 copy-start.15
  300.2 0.7 copy-start.17
  300.9 1.6 copy-start.21
  300.9 1.6 copy-start.23
  342.7 1.5 copy-start.19
  342.7 16.9 %copy-start.7 = (f32[1,512]{1,0:T(1,128)S(1)}, f32[1,512]{1,0:T(1,128)}, u32[]{:S(2)}) copy-start(f32[1,512]{1,0:T(1,128)} %constant_dynamic-slice_fusion.4) | copy-start | bytes 6148
  367.5 87.6 %copy-start.2 = (f32[64,4096]{1,0:T(8,128)S(1)}, f32[64,4096]{1,0:T(8,128)}, u32[]{:S(2)}) copy-start(f32[64,4096]{1,0:T(8,128)} %reduce-scatter.3.cloned.1.call-done) | copy-start | bytes 3145732
  455.1 2.7 copy-start.1
Sparse Core Ops, SparseCore 0:
  8.9 49.5 all-gather.5
  136.8 87.4 reduce-scatter.2
  239.2 48.2 all-gather.3
  367.7 87.4 reduce-scatter.4
where the time goes:
time: 466 us; the launch traced here: 464 us
  waiting for transfers between devices  250 us (54%)
  local copies, waits for them, and re-layouts  97.7 us (21%)
  matrix products  53.9 us (12%)
  blocking collectives  30.5 us (7%)
  other arithmetic  14.3 us (3%)
  between operations  13.7 us (3%)
    reduce_scatter x2, waiting for transfers between devices, layer(): lax.psum_scatter(jnp.dot(normed, out_local, preferred_element_type=jnp.fl...  175 us
    all_gather x2, waiting for transfers between devices, layer(): lax.all_gather(shard, 'seq', axis=0, tiled=True)  65.2 us
    dynamic_update_slice x8, local copies, waits for them, and re-layouts, layer(): lax.scan(run_block, start_state, (x_blocks, b_blocks, c_blocks, step_bloc...  42.2 us
    psum x2, blocking collectives, layer(): summed_squares = lax.psum(group_mask * own_squares[None, :], 'seq')  30.5 us
    dot_general x2, matrix products, layer(): jnp.dot(lax.all_gather(shard, 'seq', axis=0, tiled=True), own_weight, pre...  23.3 us
    dot_general x2, matrix products, layer(): jnp.dot(normed, out_local, preferred_element_type=jnp.float32)  15.9 us
    concatenate x1, local copies, waits for them, and re-layouts, on_device(): jnp.concatenate([xz_local, lax.dynamic_slice_in_dim(full_proj, b_start, S...  15.5 us
    unnamed x65, local copies, waits for them, and re-layouts  12.3 us
  transfers between devices with their start and end apart: 5, of which 5 were waited for; matrix products, arithmetic and copies ran while one was open for 7% of the time, Pallas kernels for 0%

commit v1 on v0

--- a/solution.py
+++ b/solution.py
@@ -146,7 +146,7 @@
         ).astype(jnp.float32)
         gated = mixed.reshape(length, chan_dev) * jax.nn.silu(gate_z.astype(jnp.float32))
         own_squares = jnp.sum(gated * gated, axis=1)
-        summed_squares = lax.psum(group_mask * own_squares[None, :], "seq")
+        summed_squares = jnp.sum(lax.all_gather(group_mask * own_squares[None, :], "seq"), axis=0)
         mean_square = jnp.sum(summed_squares * group_mask, axis=0) / (inner // GROUPS)
         normed = (gated * lax.rsqrt(mean_square + 1e-05)[:, None] * gain_own).astype(jnp.bfloat16)
         return lax.psum_scatter(

time: 466 us -> 466 us (level)
    psum x2 -> x0, blocking collectives: 30.5 us -> none  [layer(): summed_squares = lax.psum(group_mask * own_squares[None, :], 'seq')]
    all_gather x0 -> x2, blocking collectives: none -> 28.4 us  [layer(): lax.all_gather(group_mask * own_squares[None, :], 'seq')]
where the time goes in v1:
time: 466 us; the launch traced here: 464 us
  waiting for transfers between devices  252 us (54%)
  local copies, waits for them, and re-layouts  97.7 us (21%)
  matrix products  53.9 us (12%)
  blocking collectives  28.4 us (6%)
  other arithmetic  14.4 us (3%)
  between operations  13.7 us (3%)
    reduce_scatter x2, waiting for transfers between devices, layer(): lax.psum_scatter(jnp.dot(normed, out_local, preferred_element_type=jnp.fl...  177 us
    all_gather x2, waiting for transfers between devices, layer(): lax.all_gather(shard, 'seq', axis=0, tiled=True)  65.2 us
    dynamic_update_slice x8, local copies, waits for them, and re-layouts, layer(): lax.scan(run_block, start_state, (x_blocks, b_blocks, c_blocks, step_bloc...  42.2 us
    all_gather x2, blocking collectives, layer(): lax.all_gather(group_mask * own_squares[None, :], 'seq')  28.4 us
    dot_general x2, matrix products, layer(): jnp.dot(lax.all_gather(shard, 'seq', axis=0, tiled=True), own_weight, pre...  23.3 us
    dot_general x2, matrix products, layer(): jnp.dot(normed, out_local, preferred_element_type=jnp.float32)  15.9 us
    concatenate x1, local copies, waits for them, and re-layouts, on_device(): jnp.concatenate([xz_local, lax.dynamic_slice_in_dim(full_proj, b_start, S...  15.5 us
    unnamed x65, local copies, waits for them, and re-layouts  12.3 us
  transfers between devices with their start and end apart: 5, of which 5 were waited for; matrix products, arithmetic and copies ran while one was open for 7% of the time, Pallas kernels for 0%

profile of v1, /device:TPU:0, one launch (start us, length us, event | category | flops | bytes accessed | tf_op | source)
XLA Modules:
  0.0 464.0 jit_solution(17039927147991801097)
XLA Ops:
  7.4 9.4 %copy.112 = bf16[512,8,2,512]{3,1,2,0:T(8,128)(2,1)} copy(bf16[512,8,2,512]{3,2,1,0:T(2,128)(2,1)} %bitcast.287) | data formatting | bytes 16777216
  17.6 1.6 dynamic-slice_bitcast_fusion
  19.2 2.5 dynamic-slice_bitcast_fusion.1
  21.8 15.5 %concatenate.15 = bf16[4096,1168]{1,0:T(8,128)(2,1)} concatenate(bf16[4096,1024]{1,0:T(8,128)(2,1)} %bitcast.282, bf16[4096,64]{1,0:T(8,128)(2,1)S(1)} %get-tuple-element.256, bf16[4096,64]{1,0:T(8,128)(2,1)S(1)} %get-tuple-element.255, bf16[4096,16]{1,0:T(8,128)(2,1)S(1)} %dynamic-slice_bitcast_fusion), dimensions={1} | concatenate | bytes 19136512 | tf_op jit(solution)/shard_map/concatenate | solution.py:102
  41.7 16.9 %all-gather.6.cloned.1.call-done = bf16[1,512,4096]{2,1,0:T(8,128)(2,1)} async-done(((bf16[1,64,4096]{2,1,0:T(8,128)(2,1)}), bf16[1,512,4096]{2,1,0:T(8,128)(2,1)}) %all-gather.6.cloned.1.call-update) | async-done | bytes 4194320 | tf_op jit(solution)/shard_map/all_gather | solution.py:114
  58.6 10.6 %fusion.79 = bf16[512,1168]{0,1:T(8,128)(2,1)S(1)} fusion(bf16[4096,1168]{1,0:T(8,128)(2,1)} %concatenate.15, bf16[1,512,4096]{2,1,0:T(8,128)(2,1)} %all-gather.6.cloned.1.call-done), kind=kOutput, calls=%fused_computation.96 | convolution fusion | flops 4899545088 | bytes 14958592 | tf_op jit(solution)/shard_map/dot_general | solution.py:113
  69.2 1.5 multiply_convert_fusion.7
  73.2 38.5 %while.26 = (s32[]{:T(128)}, f32[1,16,32,64]{3,2,1,0:T(8,128)S(1)}, f32[4,128,1,16,32]{1,0,4,3,2:T(4,128)S(1)}, f32[4,128,1,16]{3,1,2,0:T(8,128)}, bf16[4,128,1,...) while((s32[]{:T(128)}, f32[1,16,32,64]{3,2,1,0:T(8,128)S(1)}, ...), condition=%wide.region_2.3_spmd.clone, body=%wide.region_0.2_spmd.clone.sunk | while | flops 37701632 | bytes 2641344 | solution.py:141
  77.3 5.3 %dynamic_update_slice.11 = f32[4,128,1,16,32]{1,0,4,3,2:T(4,128)S(1)} dynamic-update-slice(f32[4,128,1,16,32]{1,0,4,3,2:T(4,128)S(1)} %get-tuple-element.393, f32[1,128,1,16,32]{1,0,4,3,2:T(1,128)S(1)} %bitcast.288, s32[]{:T(128)} %get-tuple-element.391, s32[]{:T(128)} %constant.98.clone.1..sunk, s32[]{:T(128)} %constant.98.clone.1..sunk, s32[]{:T(128)} %constant.98.clone.1..sunk, ...) | dynamic-update-slice | bytes 524292 | tf_op jit(solution)/shard_map/while/body/jit(dynamic_update_index_in_dim)/dynamic_update_slice | solution.py:141
  86.9 5.3 %dynamic_update_slice.11 = f32[4,128,1,16,32]{1,0,4,3,2:T(4,128)S(1)} dynamic-update-slice(f32[4,128,1,16,32]{1,0,4,3,2:T(4,128)S(1)} %get-tuple-element.393, f32[1,128,1,16,32]{1,0,4,3,2:T(1,128)S(1)} %bitcast.288, s32[]{:T(128)} %get-tuple-element.391, s32[]{:T(128)} %constant.98.clone.1..sunk, s32[]{:T(128)} %constant.98.clone.1..sunk, s32[]{:T(128)} %constant.98.clone.1..sunk, ...) | dynamic-update-slice | bytes 524292 | tf_op jit(solution)/shard_map/while/body/jit(dynamic_update_index_in_dim)/dynamic_update_slice | solution.py:141
  96.5 5.3 %dynamic_update_slice.11 = f32[4,128,1,16,32]{1,0,4,3,2:T(4,128)S(1)} dynamic-update-slice(f32[4,128,1,16,32]{1,0,4,3,2:T(4,128)S(1)} %get-tuple-element.393, f32[1,128,1,16,32]{1,0,4,3,2:T(1,128)S(1)} %bitcast.288, s32[]{:T(128)} %get-tuple-element.391, s32[]{:T(128)} %constant.98.clone.1..sunk, s32[]{:T(128)} %constant.98.clone.1..sunk, s32[]{:T(128)} %constant.98.clone.1..sunk, ...) | dynamic-update-slice | bytes 524292 | tf_op jit(solution)/shard_map/while/body/jit(dynamic_update_index_in_dim)/dynamic_update_slice | solution.py:141
  106.2 5.3 %dynamic_update_slice.11 = f32[4,128,1,16,32]{1,0,4,3,2:T(4,128)S(1)} dynamic-update-slice(f32[4,128,1,16,32]{1,0,4,3,2:T(4,128)S(1)} %get-tuple-element.393, f32[1,128,1,16,32]{1,0,4,3,2:T(1,128)S(1)} %bitcast.288, s32[]{:T(128)} %get-tuple-element.391, s32[]{:T(128)} %constant.98.clone.1..sunk, s32[]{:T(128)} %constant.98.clone.1..sunk, s32[]{:T(128)} %constant.98.clone.1..sunk, ...) | dynamic-update-slice | bytes 524292 | tf_op jit(solution)/shard_map/while/body/jit(dynamic_update_index_in_dim)/dynamic_update_slice | solution.py:141
  111.8 1.5 multiply_reduce_fusion.1
  113.3 14.2 %all_gather.15 = f32[8,4,512]{2,1,0:T(4,128)S(1)} all-gather(f32[1,4,512]{2,1,0:T(4,128)S(1)} %broadcast_multiply_fusion.3), channel_id=1, replica_groups=mesh['section'=4,'seq'=8] {'seq'}, dimensions={0}, use_global_device_ids=true | all-gather | bytes 73728 | tf_op jit(solution)/shard_map/all_gather | solution.py:149
  127.6 8.0 %fusion.72 = f32[512,4096]{1,0:T(8,128)} fusion(bf16[1,512,4096]{2,1,0:T(8,128)(2,1)} %param.25, f32[512,512]{0,1:T(8,128)S(1)} %get-tuple-element.252, f32[512]{0:T(512)S(1)} %bitcast.300, f32[512]{0:T(512)S(1)} %add_rsqrt_fusion.1), kind=kOutput, calls=%fused_computation.90 | convolution fusion | flops 2148270080 | bytes 13635584 | tf_op jit(solution)/shard_map/dot_general | solution.py:153
  135.7 88.4 %reduce-scatter.3.cloned.1.call-done = f32[64,4096]{1,0:T(8,128)} async-done(((f32[512,4096]{1,0:T(8,128)}), f32[64,4096]{1,0:T(8,128)}) %reduce-scatter.3.cloned.1.call-update) | async-done | bytes 1048592 | tf_op jit(solution)/shard_map/reduce_scatter | solution.py:152
  224.0 1.3 convert_element_type.138
  225.3 3.4 collective-permute-start
  228.7 9.3 %collective-permute-done = bf16[64,4096]{1,0:T(8,128)(2,1)S(1)} collective-permute-done((bf16[64,4096]{1,0:T(8,128)(2,1)S(1)}, bf16[64,4096]{1,0:T(8,128)(2,1)S(1)}, u32[]{:S(2)}, u32[]{:S(2)}) %collective-permute-start) | collective-permute-done | bytes 524320 | tf_op jit(solution)/shard_map/ppermute | solution.py:17
  238.9 48.3 %all-gather.4.cloned.1.call-done = bf16[512,4096]{1,0:T(8,128)(2,1)} async-done(((bf16[64,4096]{1,0:T(8,128)(2,1)}), bf16[512,4096]{1,0:T(8,128)(2,1)}) %all-gather.4.cloned.1.call-update) | async-done | bytes 4194320 | tf_op jit(solution)/shard_map/all_gather | solution.py:114
  287.2 12.7 %convolution_convert_fusion = bf16[512,1168]{0,1:T(8,128)(2,1)S(1)} fusion(bf16[512,4096]{1,0:T(8,128)(2,1)} %all-gather.4.cloned.1.call-done, bf16[4096,1168]{1,0:T(8,128)(2,1)} %concatenate.15), kind=kOutput, calls=%fused_computation.94 | convolution fusion | flops 4899545088 | bytes 14958592 | tf_op jit(solution)/shard_map/dot_general | solution.py:113
  300.7 1.5 multiply_convert_fusion.6
  304.0 38.5 %while.27 = (s32[]{:T(128)}, f32[1,16,32,64]{3,2,1,0:T(8,128)S(1)}, f32[4,128,1,16,32]{1,0,4,3,2:T(4,128)S(1)}, f32[4,128,1,16]{3,1,2,0:T(8,128)}, bf16[4,128,1,...) while((s32[]{:T(128)}, f32[1,16,32,64]{3,2,1,0:T(8,128)S(1)}, ...), condition=%wide.region_9.10_spmd.clone, body=%wide.region_7.9_spmd.clone.sunk | while | flops 37701632 | bytes 2641344 | solution.py:141
  308.0 5.3 %dynamic_update_slice.12 = f32[4,128,1,16,32]{1,0,4,3,2:T(4,128)S(1)} dynamic-update-slice(f32[4,128,1,16,32]{1,0,4,3,2:T(4,128)S(1)} %get-tuple-element.423, f32[1,128,1,16,32]{1,0,4,3,2:T(1,128)S(1)} %bitcast.289, s32[]{:T(128)} %get-tuple-element.421, s32[]{:T(128)} %constant.98.clone.1..sunk.1, s32[]{:T(128)} %constant.98.clone.1..sunk.1, s32[]{:T(128)} %constant.98.clone.1..sunk.1, ...) | dynamic-update-slice | bytes 524292 | tf_op jit(solution)/shard_map/while/body/jit(dynamic_update_index_in_dim)/dynamic_update_slice | solution.py:141
  317.6 5.3 %dynamic_update_slice.12 = f32[4,128,1,16,32]{1,0,4,3,2:T(4,128)S(1)} dynamic-update-slice(f32[4,128,1,16,32]{1,0,4,3,2:T(4,128)S(1)} %get-tuple-element.423, f32[1,128,1,16,32]{1,0,4,3,2:T(1,128)S(1)} %bitcast.289, s32[]{:T(128)} %get-tuple-element.421, s32[]{:T(128)} %constant.98.clone.1..sunk.1, s32[]{:T(128)} %constant.98.clone.1..sunk.1, s32[]{:T(128)} %constant.98.clone.1..sunk.1, ...) | dynamic-update-slice | bytes 524292 | tf_op jit(solution)/shard_map/while/body/jit(dynamic_update_index_in_dim)/dynamic_update_slice | solution.py:141
  327.3 5.3 %dynamic_update_slice.12 = f32[4,128,1,16,32]{1,0,4,3,2:T(4,128)S(1)} dynamic-update-slice(f32[4,128,1,16,32]{1,0,4,3,2:T(4,128)S(1)} %get-tuple-element.423, f32[1,128,1,16,32]{1,0,4,3,2:T(1,128)S(1)} %bitcast.289, s32[]{:T(128)} %get-tuple-element.421, s32[]{:T(128)} %constant.98.clone.1..sunk.1, s32[]{:T(128)} %constant.98.clone.1..sunk.1, s32[]{:T(128)} %constant.98.clone.1..sunk.1, ...) | dynamic-update-slice | bytes 524292 | tf_op jit(solution)/shard_map/while/body/jit(dynamic_update_index_in_dim)/dynamic_update_slice | solution.py:141
  336.9 5.3 %dynamic_update_slice.12 = f32[4,128,1,16,32]{1,0,4,3,2:T(4,128)S(1)} dynamic-update-slice(f32[4,128,1,16,32]{1,0,4,3,2:T(4,128)S(1)} %get-tuple-element.423, f32[1,128,1,16,32]{1,0,4,3,2:T(1,128)S(1)} %bitcast.289, s32[]{:T(128)} %get-tuple-element.421, s32[]{:T(128)} %constant.98.clone.1..sunk.1, s32[]{:T(128)} %constant.98.clone.1..sunk.1, s32[]{:T(128)} %constant.98.clone.1..sunk.1, ...) | dynamic-update-slice | bytes 524292 | tf_op jit(solution)/shard_map/while/body/jit(dynamic_update_index_in_dim)/dynamic_update_slice | solution.py:141
  342.5 1.5 multiply_reduce_fusion
  344.1 14.2 %all_gather.17 = f32[8,4,512]{2,1,0:T(4,128)S(1)} all-gather(f32[1,4,512]{2,1,0:T(4,128)S(1)} %broadcast_multiply_fusion.2), channel_id=1, replica_groups=mesh['section'=4,'seq'=8] {'seq'}, dimensions={0}, use_global_device_ids=true | all-gather | bytes 73728 | tf_op jit(solution)/shard_map/all_gather | solution.py:149
  358.4 7.9 %fusion.70 = f32[512,4096]{1,0:T(8,128)} fusion(bf16[1,512,4096]{2,1,0:T(8,128)(2,1)} %param.25, f32[512,512]{0,1:T(8,128)S(1)} %get-tuple-element.250, f32[512]{0:T(512)S(1)} %add_rsqrt_fusion, f32[512]{0:T(512)S(1)} %bitcast.301), kind=kOutput, calls=%fused_computation.88 | convolution fusion | flops 2148270080 | bytes 13635584 | tf_op jit(solution)/shard_map/dot_general | solution.py:153
  366.3 88.4 %reduce-scatter.5.cloned.1.call-done = f32[64,4096]{1,0:T(8,128)} async-done(((f32[512,4096]{1,0:T(8,128)}), f32[64,4096]{1,0:T(8,128)}) %reduce-scatter.5.cloned.1.call-update) | async-done | bytes 1048592 | tf_op jit(solution)/shard_map/reduce_scatter | solution.py:152
  454.7 2.7 maximum_bitcast_fusion
  (224 shorter events, 46.3 us)
Async XLA Ops:
  6.5 32.8 %copy-start = (f32[1,4096]{1,0:T(1,128)S(1)}, f32[1,4096]{1,0:T(1,128)}, u32[]{:S(2)}) copy-start(f32[1,4096]{1,0:T(1,128)} %param.24) | copy-start | bytes 49156
  6.5 52.0 %all-gather.6.cloned.1.call-start = ((), (), s32[]{:S(2)}) async-start(), calls=%async_computation.5 | async-start | bytes 4718592 | tf_op jit(solution)/shard_map/all_gather | solution.py:114
  7.3 216.8 %reduce-scatter.3.cloned.1.call-start = ((), (), s32[]{:S(2)}) async-start(), calls=%async_computation.2 | async-start | bytes 9437184 | tf_op jit(solution)/shard_map/reduce_scatter | solution.py:152
  7.3 9.4 %copy-start.26 = (f32[1,128]{1,0:T(1,128)S(1)}, f32[1,128]{1,0:T(1,128)}, u32[]{:S(2)}) copy-start(f32[1,128]{1,0:T(1,128)} %param.23) | copy-start | bytes 1540
  21.8 16.1 %copy-start.24 = (f32[1,128]{1,0:T(1,128)S(1)}, f32[1,128]{1,0:T(1,128)}, u32[]{:S(2)}) copy-start(f32[1,128]{1,0:T(1,128)} %param.21) | copy-start | bytes 1540
  21.8 16.1 %copy-start.25 = (f32[1,128]{1,0:T(1,128)S(1)}, f32[1,128]{1,0:T(1,128)}, u32[]{:S(2)}) copy-start(f32[1,128]{1,0:T(1,128)} %param.22) | copy-start | bytes 1540
  37.9 33.2 %copy-start.20 = (f32[16]{0:T(128)}, f32[16]{0:T(128)S(1)}, u32[]{:S(2)}) copy-start(f32[16]{0:T(128)S(1)} %get-tuple-element.269) | copy-start | bytes 196
  37.9 33.2 %copy-start.22 = (f32[16]{0:T(128)}, f32[16]{0:T(128)S(1)}, u32[]{:S(2)}) copy-start(f32[16]{0:T(128)S(1)} %get-tuple-element.270) | copy-start | bytes 196
  40.8 28.4 %copy-start.8 = (f32[640]{0:T(1024)}, f32[640]{0:T(1024)S(1)}, u32[]{:S(2)}) copy-start(f32[640]{0:T(1024)S(1)} %pad_maximum_fusion.1) | copy-start | bytes 7684
  41.6 27.6 %copy-start.10 = (f32[640]{0:T(1024)}, f32[640]{0:T(1024)S(1)}, u32[]{:S(2)}) copy-start(f32[640]{0:T(1024)S(1)} %get-tuple-element.209) | copy-start | bytes 7684
  41.6 27.6 %copy-start.12 = (f32[640]{0:T(1024)}, f32[640]{0:T(1024)S(1)}, u32[]{:S(2)}) copy-start(f32[640]{0:T(1024)S(1)} %get-tuple-element.210) | copy-start | bytes 7684
  41.6 27.6 %copy-start.14 = (f32[640]{0:T(1024)}, f32[640]{0:T(1024)S(1)}, u32[]{:S(2)}) copy-start(f32[640]{0:T(1024)S(1)} %get-tuple-element.211) | copy-start | bytes 7684
  41.6 27.6 %copy-start.16 = (f32[640]{0:T(1024)}, f32[640]{0:T(1024)S(1)}, u32[]{:S(2)}) copy-start(f32[640]{0:T(1024)S(1)} %get-tuple-element.212) | copy-start | bytes 7684
  69.1 1.7 copy-start.4
  111.7 1.5 copy-start.18
  111.7 15.9 %copy-start.6 = (f32[1,512]{1,0:T(1,128)S(1)}, f32[1,512]{1,0:T(1,128)}, u32[]{:S(2)}) copy-start(f32[1,512]{1,0:T(1,128)} %constant_dynamic-slice_fusion.4) | copy-start | bytes 6148
  135.6 102.4 %copy-start.5 = (bf16[1,64,4096]{2,1,0:T(8,128)(2,1)S(1)}, bf16[1,64,4096]{2,1,0:T(8,128)(2,1)}, u32[]{:S(2)}) copy-start(bf16[1,64,4096]{2,1,0:T(8,128)(2,1)} %param.16) | copy-start | bytes 1572868
  135.6 151.6 %all-gather.4.cloned.1.call-start = ((), (), s32[]{:S(2)}) async-start(), calls=%async_computation.3 | async-start | bytes 4718592 | tf_op jit(solution)/shard_map/all_gather | solution.py:114
  225.3 12.7 %collective-permute-start = (bf16[64,4096]{1,0:T(8,128)(2,1)S(1)}, bf16[64,4096]{1,0:T(8,128)(2,1)S(1)}, u32[]{:S(2)}, u32[]{:S(2)}) collective-permute-start(bf16[64,4096]{1,0:T(8,128)(2,1)S(1)} %convert_element_type.138), channel_id=1, source_target_pairs={{0,8},{8,16},{16,24},{1,9},{9,17},{17,25},{2,10},{10,18},{18,26},{... | collective-permute-start | bytes 1572872 | tf_op jit(solution)/shard_map/ppermute | solution.py:17
  238.9 215.9 %reduce-scatter.5.cloned.1.call-start = ((), (), s32[]{:S(2)}) async-start(), calls=%async_computation.4 | async-start | bytes 9437184 | tf_op jit(solution)/shard_map/reduce_scatter | solution.py:152
  300.0 2.4 copy-start.3
  300.0 0.7 copy-start.9
  300.0 0.7 copy-start.11
  300.0 0.7 copy-start.13
  300.0 0.7 copy-start.15
  300.0 0.7 copy-start.17
  300.7 1.6 copy-start.21
  300.7 1.6 copy-start.23
  342.5 1.5 copy-start.19
  342.5 15.9 %copy-start.7 = (f32[1,512]{1,0:T(1,128)S(1)}, f32[1,512]{1,0:T(1,128)}, u32[]{:S(2)}) copy-start(f32[1,512]{1,0:T(1,128)} %constant_dynamic-slice_fusion.4) | copy-start | bytes 6148
  366.3 88.5 %copy-start.2 = (f32[64,4096]{1,0:T(8,128)S(1)}, f32[64,4096]{1,0:T(8,128)}, u32[]{:S(2)}) copy-start(f32[64,4096]{1,0:T(8,128)} %reduce-scatter.3.cloned.1.call-done) | copy-start | bytes 3145732
  454.7 2.7 copy-start.1
Sparse Core Ops, SparseCore 0:
  8.9 49.5 all-gather.5
  135.7 88.2 reduce-scatter.2
  239.0 48.2 all-gather.3
  366.4 88.2 reduce-scatter.4
